TPU v7x, 128 devices: a whole 4x4x4 slice. The times are simulated.
128 devices in a mesh: state: 4 (over z_hi, core), row: 32 (over z_lo, x, y).
Axes of the slice: x: 4, y: 4, z: 4 (z_hi: 2, z_lo: 2; z = z_hi * 2 + z_lo), core: 2. Of those that a mesh axis runs over, the one named last changes fastest.
Arguments:
- vectors: bfloat16 [131072, 512], P('row', 'state'), as said below
- active: int32 [8], replicated, may hold values 0 or 1
Outputs:
- orthonormal: bfloat16 [131072, 512], P('row', 'state')
Inputs may be any that keep to these rules, and one draw needn't show every extreme that they name: Each row and each column of vectors has its own scale.
All inputs are finite; a program needn't handle non-finite values.
Results may differ from a plain program's by a relative error of at most 0.00096.
Values may be sent and summed in bfloat16 or wider, within the bound.
A program may use at most 64 MiB of HBM per device.

v0:
```python
import jax
import jax.numpy as jnp
from jax import lax
from jax.sharding import PartitionSpec as P

VECS = 64
ITERS = 5


def newton_schulz(gram_matrix, total_rows):
    identity = jnp.eye(gram_matrix.shape[0], dtype=jnp.float32)
    frob_norm = jnp.sqrt(jnp.sum(gram_matrix * gram_matrix))
    current = gram_matrix / frob_norm
    inverse = identity
    for repeat in range(ITERS):
        newton_step = 0.5 * (
            3.0 * identity - jnp.dot(inverse, current, precision=lax.Precision.HIGHEST)
        )
        current = jnp.dot(current, newton_step, precision=lax.Precision.HIGHEST)
        inverse = jnp.dot(newton_step, inverse, precision=lax.Precision.HIGHEST)
    return (inverse * jnp.sqrt(total_rows / frob_norm)).astype(jnp.bfloat16)


def cross_product(left_block, right_block):
    return lax.dot_general(
        left_block, right_block, (((0,), (0,)), ((), ())), preferred_element_type=jnp.float32
    )


def shards(vectors, active):
    block_width = vectors.shape[1]
    total_rows = vectors.shape[0] * lax.axis_size("row")
    start_col = lax.axis_index("state") * block_width
    flag_all = jnp.repeat(active.astype(jnp.float32), VECS)
    flag_cols = lax.dynamic_slice_in_dim(flag_all, start_col, block_width, 0)
    masked = vectors * flag_cols.astype(jnp.bfloat16)
    gathered = lax.all_gather(masked, "state", axis=1, tiled=True)
    gram_matrix = cross_product(gathered, gathered)
    gram_matrix = lax.psum(gram_matrix, "row")
    gram_matrix = gram_matrix + jnp.diag((1.0 - flag_all) * total_rows)
    factor = newton_schulz(gram_matrix, total_rows)
    my_factor = lax.dynamic_slice_in_dim(factor, start_col, block_width, 1)
    result = jnp.dot(gathered, my_factor, preferred_element_type=jnp.float32)
    result = result + (1.0 - flag_cols) * vectors.astype(jnp.float32)
    return result.astype(jnp.bfloat16)


def solution(mesh):
    in_specs = (P("row", "state"), P())
    out_specs = P("row", "state")
    return jax.shard_map(shards, mesh=mesh, in_specs=in_specs, out_specs=out_specs, check_vma=False)
```

profile of v0, /device:TPU:0, one launch (start us, length us, event | category | flops | bytes accessed | tf_op | source)
XLA Modules:
  0.0 406.8 jit_solution(8900050890068867705)
XLA Ops:
  6.5 0.0 all-gather.2.cloned.1.call-start
  6.5 0.7 convert_element_type.16
  7.2 0.1 broadcast_in_dim.21
  7.3 0.1 reshape.11
  7.3 0.1 dynamic_slice.15
  7.4 2.3 broadcast_multiply_fusion
  9.7 0.0 all-gather.2.cloned.1.call-update
  9.7 0.0 all-reduce.2.cloned.1.call-start
  9.8 41.8 %all-gather.2.cloned.1.call-done = bf16[4096,512]{1,0:T(8,128)(2,1)} async-done(((bf16[4096,128]{1,0:T(8,128)(2,1)}), bf16[4096,512]{1,0:T(8,128)(2,1)}) %all-gather.2.cloned.1.call-update) | async-done | bytes 4194320 | tf_op jit(solution)/shard_map/all_gather | solution.py:37
  51.5 6.8 %fusion.15 = f32[512,512]{1,0:T(8,128)} fusion(bf16[4096,512]{1,0:T(8,128)(2,1)} %all-gather.2.cloned.1.call-done), kind=kOutput, calls=%fused_computation.26 | convolution fusion | flops 2147483648 | bytes 5242880 | tf_op jit(solution)/shard_map/dot_general | solution.py:25
  58.3 0.0 all-reduce.2.cloned.1.call-update
  58.4 0.1 broadcast_subtract_fusion
  58.4 310.3 %all-reduce.2.cloned.1.call-done = f32[512,512]{1,0:T(8,128)} async-done(((f32[512,512]{1,0:T(8,128)}), f32[512,512]{1,0:T(8,128)}) %all-reduce.2.cloned.1.call-update) | async-done | bytes 1048592 | tf_op jit(solution)/shard_map/psum | solution.py:39
  368.8 2.2 multiply_reduce_fusion
  371.6 0.0 copy-start.2
  371.7 2.4 fusion.5
  374.1 1.0 fusion.6
  375.1 0.0 copy-done.2
  375.1 1.9 fusion.12
  377.0 1.8 fusion.1
  378.8 1.8 fusion.17
  380.7 1.8 fusion.16
  382.6 2.0 fusion.2
  384.6 1.8 fusion.19
  386.5 1.8 fusion.18
  388.3 1.9 fusion.3
  390.2 1.8 fusion.20
  392.0 0.0 copy-start.1
  392.0 1.8 fusion.21
  394.0 0.0 copy-start
  394.0 1.9 fusion.4
  395.9 1.9 fusion.22
  397.7 0.0 copy-done.1
  397.7 0.0 copy-done
  397.7 2.2 fusion
  (1 shorter events, 0.0 us)
Async XLA Ops:
  6.5 45.0 %all-gather.2.cloned.1.call-start = ((), (), s32[]{:S(2)}) async-start(), calls=%async_computation | async-start | bytes 5242880 | tf_op jit(solution)/shard_map/all_gather | solution.py:37
  9.7 359.1 %all-reduce.2.cloned.1.call-start = ((), (), s32[]{:S(2)}) async-start(), calls=%async_computation.1 | async-start | bytes 2097152 | tf_op jit(solution)/shard_map/psum | solution.py:39
  371.6 3.4 copy-start.2
  392.0 5.7 %copy-start.1 = (bf16[4096,128]{1,0:T(8,128)(2,1)S(1)}, bf16[4096,128]{1,0:T(8,128)(2,1)}, u32[]{:S(2)}) copy-start(bf16[4096,128]{1,0:T(8,128)(2,1)} %param.2) | copy-start | bytes 3145732
  394.0 3.7 copy-start
Sparse Core Ops, SparseCore 0:
  9.8 41.6 all-gather.1
  58.5 310.2 all-reduce.1
where the time goes:
time: 407 us
  waiting for transfers between devices  352 us (86%)
  matrix products  34.9 us (9%)
  between operations  14.3 us (4%)
  other arithmetic  5.17 us (1%)
    psum x1, waiting for transfers between devices, shards(): gram_matrix = lax.psum(gram_matrix, 'row')  310 us
    all_gather x1, waiting for transfers between devices, shards(): gathered = lax.all_gather(masked, 'state', axis=1, tiled=True)  41.8 us
    dot_general x5, matrix products, newton_schulz(): jnp.dot(inverse, current, precision=lax.Precision.HIGHEST)  10 us
    dot_general x5, matrix products, newton_schulz(): inverse = jnp.dot(newton_step, inverse, precision=lax.Precision.HIGHEST)  8.37 us
  transfers between devices with their start and end apart: 2, of which 2 were waited for; matrix products, arithmetic and copies ran while one was open for 0% of the time, Pallas kernels for 0%

commit v1 on v0

--- a/solution.py
+++ b/solution.py
@@ -34,7 +34,9 @@
     flag_all = jnp.repeat(active.astype(jnp.float32), VECS)
     flag_cols = lax.dynamic_slice_in_dim(flag_all, start_col, block_width, 0)
     masked = vectors * flag_cols.astype(jnp.bfloat16)
-    gathered = lax.all_gather(masked, "state", axis=1, tiled=True)
+    gathered = jnp.concatenate(
+        lax.all_to_all(jnp.stack([masked] * lax.axis_size("state")), "state", 0, 0), axis=1
+    )
     gram_matrix = cross_product(gathered, gathered)
     gram_matrix = lax.psum(gram_matrix, "row")
     gram_matrix = gram_matrix + jnp.diag((1.0 - flag_all) * total_rows)

time: 407 us -> 421 us (1.034)
  blocking collectives: 0 us -> 54.7 us
  waiting for transfers between devices: 352 us -> 311 us
    all_to_all x0 -> x1, blocking collectives: none -> 54.7 us  [shards(): lax.all_to_all(jnp.stack([masked] * lax.axis_size('state')), 'state', 0, 0)]
    all_gather x1 -> x0, waiting for transfers between devices: 41.8 us -> none  [shards(): gathered = lax.all_gather(masked, 'state', axis=1, tiled=True)]
  transfers between devices with their start and end apart: 2 -> 1, of which waited for: 2 -> 1; matrix products, arithmetic and copies ran while one was open for 0% -> 0% of each run, Pallas kernels for 0% -> 0%
where the time goes in v1:
time: 421 us
  waiting for transfers between devices  311 us (74%)
  blocking collectives  54.7 us (13%)
  matrix products  33.9 us (8%)
  between operations  14.3 us (3%)
    psum x1, waiting for transfers between devices, shards(): gram_matrix = lax.psum(gram_matrix, 'row')  311 us
    all_to_all x1, blocking collectives, shards(): lax.all_to_all(jnp.stack([masked] * lax.axis_size('state')), 'state', 0, 0)  54.7 us
    dot_general x5, matrix products, newton_schulz(): jnp.dot(inverse, current, precision=lax.Precision.HIGHEST)  10 us
    dot_general x5, matrix products, newton_schulz(): inverse = jnp.dot(newton_step, inverse, precision=lax.Precision.HIGHEST)  8.6 us
  transfers between devices with their start and end apart: 1, of which 1 were waited for; matrix products, arithmetic and copies ran while one was open for 0% of the time, Pallas kernels for 0%

profile of v1, /device:TPU:0, one launch (start us, length us, event | category | flops | bytes accessed | tf_op | source)
XLA Modules:
  0.0 421.0 jit_solution(8834540852641004241)
XLA Ops:
  6.5 0.0 all-reduce.2.cloned.1.call-start
  6.5 0.7 convert_element_type.16
  7.2 0.1 broadcast_in_dim.21
  7.3 0.1 reshape.19
  7.3 0.1 dynamic_slice.15
  7.4 1.3 broadcast_multiply_fusion
  8.7 0.5 copy.3
  9.3 0.6 stack.2
  9.8 54.7 %all_to_all.5 = bf16[4,4096,128]{1,2,0:T(8,128)(2,1)S(1)} all-to-all(bf16[4,4096,128]{1,2,0:T(8,128)(2,1)S(1)} %stack.2), channel_id=1, replica_groups=mesh['state'=4,'row'=32] {'state'}, dimensions={0} | all-to-all | bytes 8388608 | tf_op jit(solution)/shard_map/all_to_all | solution.py:38
  64.5 0.0 copy-start
  64.5 1.9 copy-done
  66.5 3.3 fusion.15
  69.8 0.0 all-reduce.2.cloned.1.call-update
  69.8 0.1 broadcast_subtract_fusion
  69.9 310.5 %all-reduce.2.cloned.1.call-done = f32[512,512]{1,0:T(8,128)} async-done(((f32[512,512]{1,0:T(8,128)}), f32[512,512]{1,0:T(8,128)}) %all-reduce.2.cloned.1.call-update) | async-done | bytes 1048592 | tf_op jit(solution)/shard_map/psum | solution.py:41
  380.4 2.2 multiply_reduce_fusion
  383.3 0.0 copy-start.2
  383.3 2.4 fusion.5
  385.7 1.0 fusion.6
  386.7 0.0 copy-done.2
  386.7 1.9 fusion.12
  388.6 1.9 fusion.1
  390.5 1.8 fusion.17
  392.3 1.8 fusion.16
  394.2 2.0 fusion.2
  396.3 1.8 fusion.19
  398.1 1.8 fusion.18
  400.0 1.9 fusion.3
  401.8 1.8 fusion.21
  403.7 0.0 copy-start.1
  403.7 1.8 fusion.20
  405.6 1.9 fusion.4
  407.4 2.1 fusion.22
  409.6 0.0 copy-done.1
  409.6 4.5 %fusion = bf16[4096,128]{1,0:T(8,128)(2,1)} fusion(bf16[4096,512]{0,1:T(8,128)(2,1)} %bitcast.31, bf16[4096,128]{1,0:T(8,128)(2,1)S(1)} %copy-done.1, f32[128]{0:T(128)S(1)} %broadcast_subtract_fusion, f32[512,512]{1,0:T(8,128)S(1)} %fusion.22, s32[]{:T(128)S(6)} %select_n.9, f32[]{:T(128)S(6)} %sqrt.7), kind=kOutput, calls=%fused_computation.1 | convolution fusion | flops 539099136 | bytes 6554120 | tf_op jit(solution)/shard_map/dot_general | solution.py:45
  (1 shorter events, 0.0 us)
Async XLA Ops:
  6.5 373.9 %all-reduce.2.cloned.1.call-start = ((), (), s32[]{:S(2)}) async-start(), calls=%async_computation.1 | async-start | bytes 2097152 | tf_op jit(solution)/shard_map/psum | solution.py:41
  64.5 1.9 copy-start
  383.3 3.4 copy-start.2
  403.7 5.9 %copy-start.1 = (bf16[4096,128]{1,0:T(8,128)(2,1)S(1)}, bf16[4096,128]{1,0:T(8,128)(2,1)}, u32[]{:S(2)}) copy-start(bf16[4096,128]{1,0:T(8,128)(2,1)} %param.2) | copy-start | bytes 3145732
Sparse Core Ops, SparseCore 0:
  70.0 310.4 all-reduce.1
